TPU v7x, 512 devices: a whole 4x8x8 slice. The times are simulated.
512 devices in a mesh: rows: 16 (over x_lo, z), cols: 32 (over y, x_hi, core).
Axes of the slice: x: 4 (x_hi: 2, x_lo: 2; x = x_hi * 2 + x_lo), y: 8, z: 8, core: 2. Of those that a mesh axis runs over, the one named last changes fastest.
Arguments:
- tokens: bfloat16 [128, 1024, 192], P('rows', 'cols'), may hold values from -60 to 60
- region_ids: int32 [128, 1024], P('rows', 'cols'), may hold values from 0 to 2
- upper_rim: bfloat16 [4, 1024, 192], P(None, 'cols'), may hold values from -60 to 60
- upper_ids: int32 [4, 1024], P(None, 'cols'), may hold values from 0 to 2
- lower_rim: bfloat16 [4, 1024, 192], P(None, 'cols'), may hold values from -60 to 60
- lower_ids: int32 [4, 1024], P(None, 'cols'), may hold values from 0 to 2
- cotangent: bfloat16 [128, 1024, 192], P('rows', 'cols'), may hold values from -6 to 6
- qkv_weight: bfloat16 [2, 192, 576], replicated, may hold values from -0.4375 to 0.4375
- proj_weight: bfloat16 [2, 192, 192], replicated, may hold values from -0.4375 to 0.4375
- inner_weight: bfloat16 [2, 192, 768], replicated, may hold values from -0.4375 to 0.4375
- outer_weight: bfloat16 [2, 768, 192], replicated, may hold values from -0.21875 to 0.21875
- bias_table: float32 [2, 225, 6], replicated, may hold values from -4 to 400
Outputs:
- token_grad: bfloat16 [128, 1024, 192], P('rows', 'cols')
- qkv_grad: float32 [2, 192, 576], P(None, 'rows', 'cols')
- proj_grad: float32 [2, 192, 192], P(None, 'rows', 'cols')
- inner_grad: float32 [2, 192, 768], P(None, 'rows', 'cols')
- outer_grad: float32 [2, 768, 192], P(None, 'rows', 'cols')
- table_grad: float32 [2, 225, 6], replicated
All inputs are finite; a program needn't handle non-finite values.
Results may differ from a plain program's by a relative error of at most 0.03.
Values may be sent and summed in bfloat16 or wider, within the bound.
A program may use at most 64 MiB of HBM per device.

v0:
```python
import jax
import jax.numpy as jnp
from jax import lax
from jax.sharding import PartitionSpec as P

WIN = 8
HALF = 4
BIAS_LEN = 225
EPS = 1e-05
MASKED = -1000000000.0


def with_halo(block, sides, width, periodic):
    for axis, dim in sides:
        count = lax.axis_size(axis)
        forward = [(i, i + 1) for i in range(count - 1)]
        if periodic:
            forward.append((count - 1, 0))
        backward = [(target, source) for source, target in forward]
        low = lax.ppermute(
            lax.slice_in_dim(block, block.shape[dim] - width, None, axis=dim), axis, forward
        )
        high = lax.ppermute(lax.slice_in_dim(block, 0, width, axis=dim), axis, backward)
        block = jnp.concatenate([low, block, high], axis=dim)
    return block


def normalize(values):
    center = jnp.mean(values, axis=-1, keepdims=True)
    shifted = values - center
    spread = jnp.mean(shifted * shifted, axis=-1, keepdims=True)
    return shifted * lax.rsqrt(spread + EPS)


def norm_back(source, grad_norm):
    _, pullback = jax.vjp(normalize, source.astype(jnp.float32))
    return pullback(grad_norm)[0]


def by_transpose(left, right):
    return lax.dot_general(
        left, right, (((1,), (1,)), ((), ())), preferred_element_type=jnp.float32
    )


def over_rows(left, right):
    return lax.dot_general(
        left, right, (((0,), (0,)), ((), ())), preferred_element_type=jnp.float32
    )


def windows(surface):
    grid_rows, grid_cols = (surface.shape[0], surface.shape[1])
    trailing = surface.shape[2:]
    blocked = surface.reshape((grid_rows // WIN, WIN, grid_cols // WIN, WIN) + trailing)
    permute = (0, 2, 1, 3) + tuple(range(4, 4 + len(trailing)))
    return blocked.transpose(permute).reshape(
        (grid_rows // WIN * (grid_cols // WIN), WIN * WIN) + trailing
    )


def unwindows(framed, grid_rows, grid_cols):
    trailing = framed.shape[2:]
    blocked = framed.reshape((grid_rows // WIN, grid_cols // WIN, WIN, WIN) + trailing)
    permute = (0, 2, 1, 3) + tuple(range(4, 4 + len(trailing)))
    return blocked.transpose(permute).reshape((grid_rows, grid_cols) + trailing)


def relative_onehot():
    places = jnp.arange(WIN * WIN, dtype=jnp.int32)
    pos_row = places // WIN
    pos_col = places % WIN
    lookup = (
        (pos_row[:, None] - pos_row[None, :] + WIN - 1) * (2 * WIN - 1)
        + pos_col[:, None]
        - pos_col[None, :]
        + WIN
        - 1
    )
    return (lookup[:, :, None] == jnp.arange(BIAS_LEN, dtype=jnp.int32)[None, None, :]).astype(
        jnp.float32
    )


def attend(normed_win, ids_win, qkv_weight, pos_bias):
    window_count, window_size, channels = normed_win.shape
    head_count = pos_bias.shape[0]
    head_size = channels // head_count
    score_scale = head_size ** (-0.5)
    qkv_all = jnp.dot(
        normed_win.reshape(window_count * window_size, channels),
        qkv_weight,
        preferred_element_type=jnp.float32,
    )
    qkv_all = qkv_all.astype(jnp.bfloat16).reshape(
        window_count, window_size, 3, head_count, head_size
    )
    scores = jnp.einsum(
        "nqhd,nkhd->nhqk", qkv_all[:, :, 0], qkv_all[:, :, 1], preferred_element_type=jnp.float32
    )
    scores = scores * score_scale + pos_bias[None]
    same_region = ids_win[:, :, None] == ids_win[:, None, :]
    scores = jnp.where(same_region[:, None], scores, MASKED)
    row_max = jnp.max(scores, axis=-1, keepdims=True)
    exponent = jnp.exp(scores - row_max)
    attn_probs = exponent / jnp.sum(exponent, axis=-1, keepdims=True)
    attn_out = jnp.einsum(
        "nhqk,nkhd->nqhd",
        attn_probs.astype(jnp.bfloat16),
        qkv_all[:, :, 2],
        preferred_element_type=jnp.float32,
    )
    return (
        qkv_all,
        attn_probs,
        attn_out.astype(jnp.bfloat16).reshape(window_count, window_size, channels),
    )


def attend_back(normed_win, qkv_all, attn_probs, grad_out, qkv_weight):
    window_count, window_size, channels = normed_win.shape
    head_count, head_size = (qkv_all.shape[3], qkv_all.shape[4])
    score_scale = head_size ** (-0.5)
    grad_heads = grad_out.reshape(window_count, window_size, head_count, head_size)
    grad_probs = jnp.einsum(
        "nqhd,nkhd->nhqk", grad_heads, qkv_all[:, :, 2], preferred_element_type=jnp.float32
    )
    grad_scores = attn_probs * (
        grad_probs - jnp.sum(grad_probs * attn_probs, axis=-1, keepdims=True)
    )
    grad_bias = jnp.sum(grad_scores, axis=0)
    scores_low = grad_scores.astype(jnp.bfloat16)
    grad_query = (
        jnp.einsum(
            "nhqk,nkhd->nqhd", scores_low, qkv_all[:, :, 1], preferred_element_type=jnp.float32
        )
        * score_scale
    )
    grad_key = (
        jnp.einsum(
            "nhqk,nqhd->nkhd", scores_low, qkv_all[:, :, 0], preferred_element_type=jnp.float32
        )
        * score_scale
    )
    grad_value = jnp.einsum(
        "nhqk,nqhd->nkhd",
        attn_probs.astype(jnp.bfloat16),
        grad_heads,
        preferred_element_type=jnp.float32,
    )
    grad_qkv = jnp.stack([grad_query, grad_key, grad_value], axis=2).astype(jnp.bfloat16)
    grad_qkv = grad_qkv.reshape(window_count * window_size, 3 * channels)
    flattened = normed_win.reshape(window_count * window_size, channels)
    grad_norm = by_transpose(grad_qkv, qkv_weight)
    grad_weight = over_rows(flattened, grad_qkv)
    return (grad_norm.reshape(window_count, window_size, channels), grad_weight, grad_bias)


def mixer_forward(surface, region, qkv_weight, table):
    grid_rows, grid_cols = (surface.shape[0], surface.shape[1])
    normed = normalize(surface.astype(jnp.float32)).astype(jnp.bfloat16)
    pos_bias = jnp.einsum("ijb,bh->hij", relative_onehot(), table, precision=lax.Precision.HIGHEST)
    qkv_all, attn_probs, attn_out = attend(windows(normed), windows(region), qkv_weight, pos_bias)
    return (normed, qkv_all, attn_probs, unwindows(attn_out, grid_rows, grid_cols))


def mixer_backward(surface, normed, qkv_all, attn_probs, grad_mix, qkv_weight):
    grid_rows, grid_cols = (surface.shape[0], surface.shape[1])
    grad_norm, grad_weight, grad_bias = attend_back(
        windows(normed), qkv_all, attn_probs, windows(grad_mix), qkv_weight
    )
    grad_surface = norm_back(surface, unwindows(grad_norm, grid_rows, grid_cols))
    grad_table = jnp.einsum(
        "ijb,hij->bh", relative_onehot(), grad_bias, precision=lax.Precision.HIGHEST
    )
    return (grad_surface, grad_weight, grad_table)


def channel_forward(middle, inner_w, outer_w):
    normed = normalize(middle.astype(jnp.float32)).astype(jnp.bfloat16)
    hidden_pre = jnp.dot(normed, inner_w, preferred_element_type=jnp.float32)
    hidden_act = jax.nn.gelu(hidden_pre, approximate=False).astype(jnp.bfloat16)
    output = (
        middle.astype(jnp.float32)
        + jnp.dot(hidden_act, outer_w, preferred_element_type=jnp.float32)
    ).astype(jnp.bfloat16)
    return (normed, hidden_pre, hidden_act, output)


def channel_backward(middle, normed, hidden_pre, hidden_act, grad_out, inner_w, outer_w):
    grad_act = by_transpose(grad_out, outer_w)
    grad_outer = over_rows(hidden_act, grad_out)
    _, pullback = jax.vjp(lambda inputs: jax.nn.gelu(inputs, approximate=False), hidden_pre)
    grad_pre = pullback(grad_act)[0].astype(jnp.bfloat16)
    grad_norm = by_transpose(grad_pre, inner_w)
    grad_inner = over_rows(normed, grad_pre)
    grad_middle = (grad_out.astype(jnp.float32) + norm_back(middle, grad_norm)).astype(jnp.bfloat16)
    return (grad_middle, grad_inner, grad_outer)


def fold_rims(grad_ext):
    col_edges = jnp.concatenate([grad_ext[:, :HALF], grad_ext[:, -HALF:]], axis=1)
    col_recv = with_halo(col_edges.astype(jnp.bfloat16), (("cols", 1),), HALF, True).astype(
        col_edges.dtype
    )
    center = grad_ext[:, HALF:-HALF]
    center = jnp.concatenate(
        [
            center[:, :HALF] + col_recv[:, :HALF],
            center[:, HALF:-HALF],
            center[:, -HALF:] + col_recv[:, -HALF:],
        ],
        axis=1,
    )
    row_edges = jnp.concatenate([center[:HALF], center[-HALF:]], axis=0)
    row_recv = with_halo(row_edges.astype(jnp.bfloat16), (("rows", 0),), HALF, False).astype(
        row_edges.dtype
    )
    interior = center[HALF:-HALF]
    return jnp.concatenate(
        [
            interior[:HALF] + row_recv[:HALF],
            interior[HALF:-HALF],
            interior[-HALF:] + row_recv[-HALF:],
        ],
        axis=0,
    )


def reduce_grads(qkv_term, proj_term, inner_term, outer_term):
    row_count = lax.axis_size("rows")
    col_count = lax.axis_size("cols")
    tile_count = row_count * col_count
    reduced = (
        lax.psum_scatter(
            qkv_term.astype(jnp.bfloat16), "cols", scatter_dimension=1, tiled=True
        ).astype(jnp.float32),
        lax.psum_scatter(
            proj_term.astype(jnp.bfloat16), "cols", scatter_dimension=1, tiled=True
        ).astype(jnp.float32),
        lax.psum_scatter(
            inner_term.astype(jnp.bfloat16), "cols", scatter_dimension=1, tiled=True
        ).astype(jnp.float32),
        lax.psum_scatter(
            outer_term.astype(jnp.bfloat16), "cols", scatter_dimension=1, tiled=True
        ).astype(jnp.float32),
    )
    reduced = (
        lax.psum_scatter(
            reduced[0].astype(jnp.bfloat16), "rows", scatter_dimension=0, tiled=True
        ).astype(jnp.float32),
        lax.psum_scatter(
            reduced[1].astype(jnp.bfloat16), "rows", scatter_dimension=0, tiled=True
        ).astype(jnp.float32),
        lax.psum_scatter(
            reduced[2].astype(jnp.bfloat16), "rows", scatter_dimension=0, tiled=True
        ).astype(jnp.float32),
        lax.psum_scatter(
            reduced[3].astype(jnp.bfloat16), "rows", scatter_dimension=0, tiled=True
        ).astype(jnp.float32),
    )
    return tuple((section / tile_count for section in reduced))


def local(
    tokens,
    region_ids,
    upper_rim,
    upper_ids,
    lower_rim,
    lower_ids,
    cotangent,
    qkv_weight,
    proj_weight,
    inner_weight,
    outer_weight,
    bias_table,
):
    tile_rows, tile_cols, channels = tokens.shape
    row_index = lax.axis_index("rows")
    row_count = lax.axis_size("rows")
    tile_count = row_count * lax.axis_size("cols")
    normed_one, qkv_one, probs_one, mix_one = mixer_forward(
        tokens, region_ids, qkv_weight[0], bias_table[0]
    )
    mix_flat_one = mix_one.reshape(tile_rows * tile_cols, channels)
    middle_one = (
        tokens.reshape(-1, channels).astype(jnp.float32)
        + jnp.dot(mix_flat_one, proj_weight[0], preferred_element_type=jnp.float32)
    ).astype(jnp.bfloat16)
    chan_one = channel_forward(middle_one, inner_weight[0], outer_weight[0])
    first_out = chan_one[3].reshape(tile_rows, tile_cols, channels)
    region_low = region_ids.astype(jnp.bfloat16)
    row_ext, row_ids = (
        with_halo(first_out, (("rows", 0),), HALF, False),
        with_halo(region_low, (("rows", 0),), HALF, False),
    )
    at_top = row_index == 0
    at_bottom = row_index == row_count - 1
    row_ext = jnp.concatenate(
        [
            jnp.where(at_top, upper_rim, row_ext[:HALF]),
            row_ext[HALF:-HALF],
            jnp.where(at_bottom, lower_rim, row_ext[-HALF:]),
        ],
        axis=0,
    )
    row_ids = jnp.concatenate(
        [
            jnp.where(at_top, upper_ids.astype(jnp.bfloat16), row_ids[:HALF]),
            row_ids[HALF:-HALF],
            jnp.where(at_bottom, lower_ids.astype(jnp.bfloat16), row_ids[-HALF:]),
        ],
        axis=0,
    )
    extended, ext_ids = (
        with_halo(row_ext, (("cols", 1),), HALF, True),
        with_halo(row_ids, (("cols", 1),), HALF, True),
    )
    ext_region = ext_ids.astype(jnp.int32)
    normed_two, qkv_two, probs_two, mix_ext = mixer_forward(
        extended, ext_region, qkv_weight[1], bias_table[1]
    )
    mix_flat_two = mix_ext[HALF : HALF + tile_rows, HALF : HALF + tile_cols].reshape(
        tile_rows * tile_cols, channels
    )
    middle_two = (
        chan_one[3].astype(jnp.float32)
        + jnp.dot(mix_flat_two, proj_weight[1], preferred_element_type=jnp.float32)
    ).astype(jnp.bfloat16)
    chan_two = channel_forward(middle_two, inner_weight[1], outer_weight[1])
    grad_out = cotangent.reshape(-1, channels)
    grad_mid_two, inner_two, outer_two = channel_backward(
        middle_two,
        chan_two[0],
        chan_two[1],
        chan_two[2],
        grad_out,
        inner_weight[1],
        outer_weight[1],
    )
    proj_two = over_rows(mix_flat_two, grad_mid_two)
    grad_mix_two = (
        by_transpose(grad_mid_two, proj_weight[1])
        .astype(jnp.bfloat16)
        .reshape(tile_rows, tile_cols, channels)
    )
    grad_mix_ext = jnp.pad(grad_mix_two, ((HALF, HALF), (HALF, HALF), (0, 0)))
    grad_ext, qkv_two_grad, table_two = mixer_backward(
        extended, normed_two, qkv_two, probs_two, grad_mix_ext, qkv_weight[1]
    )
    folded = fold_rims(grad_ext)
    grad_first = (
        grad_mid_two.reshape(tile_rows, tile_cols, channels).astype(jnp.float32) + folded
    ).astype(jnp.bfloat16)
    summed_two = reduce_grads(qkv_two_grad, proj_two, inner_two, outer_two)
    grad_mid_one, inner_one, outer_one = channel_backward(
        middle_one,
        chan_one[0],
        chan_one[1],
        chan_one[2],
        grad_first.reshape(-1, channels),
        inner_weight[0],
        outer_weight[0],
    )
    proj_one = over_rows(mix_flat_one, grad_mid_one)
    grad_mix_one = (
        by_transpose(grad_mid_one, proj_weight[0])
        .astype(jnp.bfloat16)
        .reshape(tile_rows, tile_cols, channels)
    )
    grad_tokens, qkv_one_grad, table_one = mixer_backward(
        tokens, normed_one, qkv_one, probs_one, grad_mix_one, qkv_weight[0]
    )
    token_grad = (
        grad_mid_one.reshape(tile_rows, tile_cols, channels).astype(jnp.float32) + grad_tokens
    ).astype(jnp.bfloat16)
    summed_one = reduce_grads(qkv_one_grad, proj_one, inner_one, outer_one)
    table_sum = lax.psum(jnp.stack([table_one, table_two]), ("rows", "cols"))
    qkv_grad = jnp.stack([summed_one[0], summed_two[0]])
    proj_grad = jnp.stack([summed_one[1], summed_two[1]])
    inner_grad = jnp.stack([summed_one[2], summed_two[2]])
    outer_grad = jnp.stack([summed_one[3], summed_two[3]])
    return (token_grad, qkv_grad, proj_grad, inner_grad, outer_grad, table_sum / tile_count)


def solution(mesh):
    return jax.shard_map(
        local,
        mesh=mesh,
        in_specs=(
            P("rows", "cols", None),
            P("rows", "cols"),
            P(None, "cols", None),
            P(None, "cols"),
            P(None, "cols", None),
            P(None, "cols"),
            P("rows", "cols", None),
            P(),
            P(),
            P(),
            P(),
            P(),
        ),
        out_specs=(
            P("rows", "cols", None),
            P(None, "rows", "cols"),
            P(None, "rows", "cols"),
            P(None, "rows", "cols"),
            P(None, "rows", "cols"),
            P(),
        ),
        check_vma=False,
    )
```

profile of v0, /device:TPU:16, one launch (start us, length us, event | category | flops | bytes accessed | tf_op | source)
XLA Modules:
  0.0 740.8 jit_solution(4633801604680968060)
XLA Ops:
  8.5 4.8 collective-permute-start.4
  22.0 2.6 fusion.29
  27.7 2.9 multiply_convert_fusion.1
  33.3 5.2 collective-permute-start
  38.6 2.6 fusion.30
  44.7 6.0 collective-permute-start.7
  52.6 4.1 collective-permute-start.2
  56.7 3.9 collective-permute-start.3
  64.6 3.2 reshape.352
  69.5 2.5 fusion.136
  73.2 2.3 fusion.23
  78.5 2.8 fusion.47
  85.6 2.3 fusion.24
  91.9 2.5 copy.166
  94.4 4.0 copy.147
  98.4 5.6 convert_element_type.304
  104.0 2.6 multiply_reduce_fusion.2
  110.8 2.3 convolution_convert_fusion.9
  115.4 3.2 collective-permute-start.8
  118.7 4.7 collective-permute-start.9
  125.2 4.7 collective-permute-start.10
  132.0 6.0 collective-permute-done.11
  146.3 68.5 %fusion.122 = (bf16[192,24]{0,1:T(8,128)(2,1)S(1)}, bf16[192,24]{0,1:T(8,128)(2,1)S(1)}, bf16[192,8]{0,1:T(8,128)(2,1)S(1)}, bf16[192,8]{0,1:T(8,128)(2,1)S(1)},...) fusion(bf16[192,576]{0,1:T(8,128)(2,1)} %convolution_convert_fusion.9, ...), kind=kCustom, calls=%all-reduce-scatter.6 | all-reduce-scatter fusion | flops 786434 | bytes 1230848
  214.8 20.4 %collective-permute-start.51 = (bf16[768,6]{0,1:T(8,128)(2,1)S(1)}, bf16[768,6]{0,1:T(8,128)(2,1)S(1)}, u32[]{:S(2)}, u32[]{:S(2)}) collective-permute-start(bf16[768,6]{0,1:T(8,128)(2,1)S(1)} %slice.212), channel_id=1, source_target_pairs={{0,8},{1,9},{2,10},{3,11},{4,12},{5,13},{6,14},{7,15},{8,16},{9,17... | collective-permute-start | bytes 27656
  243.0 4.6 collective-permute-start.46
  256.0 2.2 collective-permute-start.45
  268.8 3.1 collective-permute-start.54
  271.9 3.3 collective-permute-start.53
  279.9 2.8 collective-permute-done.52
  304.3 4.6 collective-permute-start.38
  308.9 2.2 collective-permute-start.37
  313.2 4.2 collective-permute-start.34
  321.4 104.6 %psum.7 = f32[2,225,6]{1,2,0:T(8,128)S(1)} all-reduce(f32[2,225,6]{1,2,0:T(8,128)S(1)} %pad_maximum_fusion.16), channel_id=1, replica_groups=mesh['rows'=16,'cols'=32] {'rows','cols'}, use_global_device_ids=true, to_apply=%region_40.41 | all-reduce | flops 2700 | bytes 21600 | tf_op jit(solution)/shard_map/psum | solution.py:379
  426.0 3.2 collective-permute-start.31
  431.1 4.8 collective-permute-start.29
  437.9 4.4 collective-permute-start.27
  443.7 5.6 collective-permute-start.26
  449.3 3.9 collective-permute-start.25
  457.2 2.8 collective-permute-start.22
  460.9 2.8 collective-permute-start.21
  465.6 3.3 collective-permute-start.18
  478.3 2.4 collective-permute-start.14
  480.8 3.1 collective-permute-start.13
  485.9 2.9 collective-permute-done.13
  488.8 2.5 collective-permute-done.12
  494.6 51.3 %reduce-scatter.29.cloned.1.call-done = bf16[192,24]{0,1:T(8,128)(2,1)} async-done(((bf16[192,768]{0,1:T(8,128)(2,1)}), bf16[192,24]{0,1:T(8,128)(2,1)}) %reduce-scatter.29.cloned.1.call-update) | async-done | bytes 9232 | tf_op jit(solution)/shard_map/reduce_scatter | solution.py:241
  545.9 121.3 %reduce-scatter.27.cloned.1.call-done = bf16[192,24]{0,1:T(8,128)(2,1)} async-done(((bf16[192,768]{0,1:T(8,128)(2,1)}), bf16[192,24]{0,1:T(8,128)(2,1)}) %reduce-scatter.27.cloned.1.call-update) | async-done | bytes 9232 | tf_op jit(solution)/shard_map/reduce_scatter | solution.py:241
  667.2 64.4 %all-reduce.19 = (bf16[192,18]{0,1:T(8,128)(2,1)S(1)}, bf16[192,18]{0,1:T(8,128)(2,1)S(1)}, bf16[192,6]{0,1:T(8,128)(2,1)S(1)}, bf16[192,6]{0,1:T(8,128)(2,1)S(1...) all-reduce(bf16[192,18]{0,1:T(8,128)(2,1)S(1)} %constant_dynamic-sl, ...), channel_id=5, replica_groups=mesh['rows'=16,'cols'=32] {'rows'}, use_global_device_ids=true, to_apply=%region_25.26.clone | all-reduce | flops 18432 | bytes 73728
  (432 shorter events, 141.9 us)
Async XLA Ops:
  7.2 485.2 %reduce-scatter.31.cloned.1.call-start = ((), (), s32[]{:S(2)}) async-start(), calls=%async_computation.6 | async-start | bytes 208896
  8.5 33.5 %collective-permute-start.4 = (bf16[4,32]{1,0:T(4,128)(2,1)}, bf16[4,32]{1,0:T(4,128)(2,1)}, u32[]{:S(2)}, u32[]{:S(2)}) collective-permute-start(bf16[4,32]{1,0:T(4,128)(2,1)} %get-tuple-element.76), channel_id=1, source_target_pairs={{0,32},{32,64},{64,96},{96,128},{128,160},{160,192},{192,224},{224... | collective-permute-start | bytes 776 | tf_op jit(solution)/shard_map/ppermute | solution.py:20
  13.4 28.6 %collective-permute-start.5 = (bf16[4,32]{1,0:T(4,128)(2,1)}, bf16[4,32]{1,0:T(4,128)(2,1)}, u32[]{:S(2)}, u32[]{:S(2)}) collective-permute-start(bf16[4,32]{1,0:T(4,128)(2,1)} %get-tuple-element.77), channel_id=1, source_target_pairs={{32,0},{64,32},{96,64},{128,96},{160,128},{192,160},{224,192},{256... | collective-permute-start | bytes 776 | tf_op jit(solution)/shard_map/ppermute | solution.py:23
  31.9 20.6 %collective-permute-start.1 = (bf16[4,32,192]{2,1,0:T(8,128)(2,1)S(1)}, bf16[4,32,192]{2,1,0:T(8,128)(2,1)S(1)}, u32[]{:S(2)}, u32[]{:S(2)}) collective-permute-start(bf16[4,32,192]{2,1,0:T(8,128)(2,1)S(1)} %bitcast.340), channel_id=1, source_target_pairs={{32,0},{64,32},{96,64},{128,96},{160,128},{192,160},{224,192},{256... | collective-permute-start | bytes 147464 | tf_op jit(solution)/shard_map/ppermute | solution.py:23
  33.3 19.3 %collective-permute-start = (bf16[4,32,192]{2,1,0:T(8,128)(2,1)S(1)}, bf16[4,32,192]{2,1,0:T(8,128)(2,1)S(1)}, u32[]{:S(2)}, u32[]{:S(2)}) collective-permute-start(bf16[4,32,192]{2,1,0:T(8,128)(2,1)S(1)} %bitcast.341), channel_id=1, source_target_pairs={{0,32},{32,64},{64,96},{96,128},{128,160},{160,192},{192,224},{224... | collective-permute-start | bytes 147464 | tf_op jit(solution)/shard_map/ppermute | solution.py:20
  42.8 8.8 %collective-permute-start.6 = (bf16[16,4]{1,0:T(8,128)(2,1)S(1)}, bf16[16,4]{1,0:T(8,128)(2,1)S(1)}, u32[]{:S(2)}, u32[]{:S(2)}) collective-permute-start(bf16[16,4]{1,0:T(8,128)(2,1)S(1)} %get-tuple-element.74), channel_id=1, source_target_pairs={{0,1},{1,2},{2,3},{3,4},{4,5},{5,6},{6,7},{7,8},{8,9},{9,10},{10,1... | collective-permute-start | bytes 392 | tf_op jit(solution)/shard_map/ppermute | solution.py:20
  52.6 8.8 %collective-permute-start.2 = (bf16[16,4,192]{2,1,0:T(4,128)(2,1)S(1)}, bf16[16,4,192]{2,1,0:T(4,128)(2,1)S(1)}, u32[]{:S(2)}, u32[]{:S(2)}) collective-permute-start(bf16[16,4,192]{2,1,0:T(4,128)(2,1)S(1)} %get-tuple-element.66), channel_id=1, source_target_pairs={{0,1},{1,2},{2,3},{3,4},{4,5},{5,6},{6,7},{7,8},{8,9},{9,10},{10,1... | collective-permute-start | bytes 73736 | tf_op jit(solution)/shard_map/ppermute | solution.py:20
  115.4 8.8 %collective-permute-start.8 = (bf16[16,4,192]{2,1,0:T(4,128)(2,1)S(1)}, bf16[16,4,192]{2,1,0:T(4,128)(2,1)S(1)}, u32[]{:S(2)}, u32[]{:S(2)}) collective-permute-start(bf16[16,4,192]{2,1,0:T(4,128)(2,1)S(1)} %get-tuple-element.62), channel_id=1, source_target_pairs={{0,1},{1,2},{2,3},{3,4},{4,5},{5,6},{6,7},{7,8},{8,9},{9,10},{10,1... | collective-permute-start | bytes 73736 | tf_op jit(solution)/shard_map/ppermute | solution.py:20
  214.8 28.2 %collective-permute-start.51 = (bf16[768,6]{0,1:T(8,128)(2,1)S(1)}, bf16[768,6]{0,1:T(8,128)(2,1)S(1)}, u32[]{:S(2)}, u32[]{:S(2)}) collective-permute-start(bf16[768,6]{0,1:T(8,128)(2,1)S(1)} %slice.212), channel_id=1, source_target_pairs={{0,8},{1,9},{2,10},{3,11},{4,12},{5,13},{6,14},{7,15},{8,16},{9,17... | collective-permute-start | bytes 27656
  235.2 16.9 %collective-permute-start.50 = (bf16[768,8]{0,1:T(8,128)(2,1)S(1)}, bf16[768,8]{0,1:T(8,128)(2,1)S(1)}, u32[]{:S(2)}, u32[]{:S(2)}) collective-permute-start(bf16[768,8]{0,1:T(8,128)(2,1)S(1)} %get-tuple-element.41), channel_id=1, source_target_pairs={{0,7},{1,8},{2,9},{3,10},{4,11},{5,12},{6,13},{7,14},{8,15},{9,16}... | collective-permute-start | bytes 36872
  237.2 16.9 %collective-permute-start.49 = (bf16[768,8]{0,1:T(8,128)(2,1)S(1)}, bf16[768,8]{0,1:T(8,128)(2,1)S(1)}, u32[]{:S(2)}, u32[]{:S(2)}) collective-permute-start(bf16[768,8]{0,1:T(8,128)(2,1)S(1)} %get-tuple-element.41), channel_id=1, source_target_pairs={{0,6},{1,7},{2,8},{3,9},{4,10},{5,11},{6,12},{7,13},{8,14},{9,15},... | collective-permute-start | bytes 36872
  239.1 16.9 %collective-permute-start.48 = (bf16[768,8]{0,1:T(8,128)(2,1)S(1)}, bf16[768,8]{0,1:T(8,128)(2,1)S(1)}, u32[]{:S(2)}, u32[]{:S(2)}) collective-permute-start(bf16[768,8]{0,1:T(8,128)(2,1)S(1)} %get-tuple-element.41), channel_id=1, source_target_pairs={{0,5},{1,6},{2,7},{3,8},{4,9},{5,10},{6,11},{7,12},{8,13},{9,14},{... | collective-permute-start | bytes 36872
  241.0 17.2 %collective-permute-start.47 = (bf16[768,8]{0,1:T(8,128)(2,1)S(1)}, bf16[768,8]{0,1:T(8,128)(2,1)S(1)}, u32[]{:S(2)}, u32[]{:S(2)}) collective-permute-start(bf16[768,8]{0,1:T(8,128)(2,1)S(1)} %get-tuple-element.41), channel_id=1, source_target_pairs={{0,4},{1,5},{2,6},{3,7},{4,8},{5,9},{6,10},{7,11},{8,12},{9,13},{1... | collective-permute-start | bytes 36872
  243.0 17.2 %collective-permute-start.46 = (bf16[768,8]{0,1:T(8,128)(2,1)S(1)}, bf16[768,8]{0,1:T(8,128)(2,1)S(1)}, u32[]{:S(2)}, u32[]{:S(2)}) collective-permute-start(bf16[768,8]{0,1:T(8,128)(2,1)S(1)} %get-tuple-element.41), channel_id=1, source_target_pairs={{0,3},{1,4},{2,5},{3,6},{4,7},{5,8},{6,9},{7,10},{8,11},{9,12},{10... | collective-permute-start | bytes 36872
  252.1 19.8 %collective-permute-start.58 = (bf16[768,8]{0,1:T(8,128)(2,1)S(1)}, bf16[768,8]{0,1:T(8,128)(2,1)S(1)}, u32[]{:S(2)}, u32[]{:S(2)}) collective-permute-start(bf16[768,8]{0,1:T(8,128)(2,1)S(1)} %get-tuple-element.40), channel_id=1, source_target_pairs={{0,7},{1,8},{2,9},{3,10},{4,11},{5,12},{6,13},{7,14},{8,15},{9,16}... | collective-permute-start | bytes 36872
  254.0 21.2 %collective-permute-start.57 = (bf16[768,8]{0,1:T(8,128)(2,1)S(1)}, bf16[768,8]{0,1:T(8,128)(2,1)S(1)}, u32[]{:S(2)}, u32[]{:S(2)}) collective-permute-start(bf16[768,8]{0,1:T(8,128)(2,1)S(1)} %get-tuple-element.40), channel_id=1, source_target_pairs={{0,6},{1,7},{2,8},{3,9},{4,10},{5,11},{6,12},{7,13},{8,14},{9,15},... | collective-permute-start | bytes 36872
  264.0 14.2 %collective-permute-start.56 = (bf16[768,8]{0,1:T(8,128)(2,1)S(1)}, bf16[768,8]{0,1:T(8,128)(2,1)S(1)}, u32[]{:S(2)}, u32[]{:S(2)}) collective-permute-start(bf16[768,8]{0,1:T(8,128)(2,1)S(1)} %get-tuple-element.40), channel_id=1, source_target_pairs={{0,5},{1,6},{2,7},{3,8},{4,9},{5,10},{6,11},{7,12},{8,13},{9,14},{... | collective-permute-start | bytes 36872
  265.9 12.2 %collective-permute-start.55 = (bf16[768,8]{0,1:T(8,128)(2,1)S(1)}, bf16[768,8]{0,1:T(8,128)(2,1)S(1)}, u32[]{:S(2)}, u32[]{:S(2)}) collective-permute-start(bf16[768,8]{0,1:T(8,128)(2,1)S(1)} %get-tuple-element.40), channel_id=1, source_target_pairs={{0,4},{1,5},{2,6},{3,7},{4,8},{5,9},{6,10},{7,11},{8,12},{9,13},{1... | collective-permute-start | bytes 36872
  268.8 9.4 %collective-permute-start.54 = (bf16[768,8]{0,1:T(8,128)(2,1)S(1)}, bf16[768,8]{0,1:T(8,128)(2,1)S(1)}, u32[]{:S(2)}, u32[]{:S(2)}) collective-permute-start(bf16[768,8]{0,1:T(8,128)(2,1)S(1)} %get-tuple-element.40), channel_id=1, source_target_pairs={{0,3},{1,4},{2,5},{3,6},{4,7},{5,8},{6,9},{7,10},{8,11},{9,12},{10... | collective-permute-start | bytes 36872
  278.1 215.1 %reduce-scatter.33.cloned.1.call-start = ((), (), s32[]{:S(2)}) async-start(), calls=%async_computation.7 | async-start | bytes 208896
  284.5 261.4 %reduce-scatter.29.cloned.1.call-start = ((), (), s32[]{:S(2)}) async-start(), calls=%async_computation.5 | async-start | bytes 405504 | tf_op jit(solution)/shard_map/reduce_scatter | solution.py:241
  286.2 381.0 %reduce-scatter.27.cloned.1.call-start = ((), (), s32[]{:S(2)}) async-start(), calls=%async_computation.4 | async-start | bytes 405504 | tf_op jit(solution)/shard_map/reduce_scatter | solution.py:241
  287.5 21.5 %collective-permute-start.42 = (bf16[192,8]{0,1:T(8,128)(2,1)S(1)}, bf16[192,8]{0,1:T(8,128)(2,1)S(1)}, u32[]{:S(2)}, u32[]{:S(2)}) collective-permute-start(bf16[192,8]{0,1:T(8,128)(2,1)S(1)} %get-tuple-element.38), channel_id=1, source_target_pairs={{0,7},{1,8},{2,9},{3,10},{4,11},{5,12},{6,13},{7,14},{8,15},{9,16}... | collective-permute-start | bytes 9224
  289.5 21.6 %collective-permute-start.41 = (bf16[192,8]{0,1:T(8,128)(2,1)S(1)}, bf16[192,8]{0,1:T(8,128)(2,1)S(1)}, u32[]{:S(2)}, u32[]{:S(2)}) collective-permute-start(bf16[192,8]{0,1:T(8,128)(2,1)S(1)} %get-tuple-element.38), channel_id=1, source_target_pairs={{0,6},{1,7},{2,8},{3,9},{4,10},{5,11},{6,12},{7,13},{8,14},{9,15},... | collective-permute-start | bytes 9224
  291.4 21.8 %collective-permute-start.40 = (bf16[192,8]{0,1:T(8,128)(2,1)S(1)}, bf16[192,8]{0,1:T(8,128)(2,1)S(1)}, u32[]{:S(2)}, u32[]{:S(2)}) collective-permute-start(bf16[192,8]{0,1:T(8,128)(2,1)S(1)} %get-tuple-element.38), channel_id=1, source_target_pairs={{0,5},{1,6},{2,7},{3,8},{4,9},{5,10},{6,11},{7,12},{8,13},{9,14},{... | collective-permute-start | bytes 9224
  302.3 15.1 %collective-permute-start.39 = (bf16[192,8]{0,1:T(8,128)(2,1)S(1)}, bf16[192,8]{0,1:T(8,128)(2,1)S(1)}, u32[]{:S(2)}, u32[]{:S(2)}) collective-permute-start(bf16[192,8]{0,1:T(8,128)(2,1)S(1)} %get-tuple-element.38), channel_id=1, source_target_pairs={{0,4},{1,5},{2,6},{3,7},{4,8},{5,9},{6,10},{7,11},{8,12},{9,13},{1... | collective-permute-start | bytes 9224
  304.3 15.1 %collective-permute-start.38 = (bf16[192,8]{0,1:T(8,128)(2,1)S(1)}, bf16[192,8]{0,1:T(8,128)(2,1)S(1)}, u32[]{:S(2)}, u32[]{:S(2)}) collective-permute-start(bf16[192,8]{0,1:T(8,128)(2,1)S(1)} %get-tuple-element.38), channel_id=1, source_target_pairs={{0,3},{1,4},{2,5},{3,6},{4,7},{5,8},{6,9},{7,10},{8,11},{9,12},{10... | collective-permute-start | bytes 9224
  308.9 117.0 %collective-permute-start.37 = (bf16[192,8]{0,1:T(8,128)(2,1)S(1)}, bf16[192,8]{0,1:T(8,128)(2,1)S(1)}, u32[]{:S(2)}, u32[]{:S(2)}) collective-permute-start(bf16[192,8]{0,1:T(8,128)(2,1)S(1)} %get-tuple-element.38), channel_id=1, source_target_pairs={{0,2},{1,3},{2,4},{3,5},{4,6},{5,7},{6,8},{7,9},{8,10},{9,11},{10,... | collective-permute-start | bytes 9224
  311.1 118.1 %collective-permute-start.36 = (bf16[192,8]{0,1:T(8,128)(2,1)S(1)}, bf16[192,8]{0,1:T(8,128)(2,1)S(1)}, u32[]{:S(2)}, u32[]{:S(2)}) collective-permute-start(bf16[192,8]{0,1:T(8,128)(2,1)S(1)} %get-tuple-element.38), channel_id=1, source_target_pairs={{0,1},{1,2},{2,3},{3,4},{4,5},{5,6},{6,7},{7,8},{8,9},{9,10},{10,1... | collective-permute-start | bytes 9224
  313.2 117.9 %collective-permute-start.34 = (bf16[192,8]{0,1:T(8,128)(2,1)S(1)}, bf16[192,8]{0,1:T(8,128)(2,1)S(1)}, u32[]{:S(2)}, u32[]{:S(2)}) collective-permute-start(bf16[192,8]{0,1:T(8,128)(2,1)S(1)} %get-tuple-element.39), channel_id=1, source_target_pairs={{0,7},{1,8},{2,9},{3,10},{4,11},{5,12},{6,13},{7,14},{8,15},{9,16}... | collective-permute-start | bytes 9224
  317.5 118.5 %collective-permute-start.33 = (bf16[192,8]{0,1:T(8,128)(2,1)S(1)}, bf16[192,8]{0,1:T(8,128)(2,1)S(1)}, u32[]{:S(2)}, u32[]{:S(2)}) collective-permute-start(bf16[192,8]{0,1:T(8,128)(2,1)S(1)} %get-tuple-element.39), channel_id=1, source_target_pairs={{0,6},{1,7},{2,8},{3,9},{4,10},{5,11},{6,12},{7,13},{8,14},{9,15},... | collective-permute-start | bytes 9224
  319.4 118.5 %collective-permute-start.32 = (bf16[192,8]{0,1:T(8,128)(2,1)S(1)}, bf16[192,8]{0,1:T(8,128)(2,1)S(1)}, u32[]{:S(2)}, u32[]{:S(2)}) collective-permute-start(bf16[192,8]{0,1:T(8,128)(2,1)S(1)} %get-tuple-element.39), channel_id=1, source_target_pairs={{0,5},{1,6},{2,7},{3,8},{4,9},{5,10},{6,11},{7,12},{8,13},{9,14},{... | collective-permute-start | bytes 9224
  426.0 17.8 %collective-permute-start.31 = (bf16[192,8]{0,1:T(8,128)(2,1)S(1)}, bf16[192,8]{0,1:T(8,128)(2,1)S(1)}, u32[]{:S(2)}, u32[]{:S(2)}) collective-permute-start(bf16[192,8]{0,1:T(8,128)(2,1)S(1)} %get-tuple-element.39), channel_id=1, source_target_pairs={{0,4},{1,5},{2,6},{3,7},{4,8},{5,9},{6,10},{7,11},{8,12},{9,13},{1... | collective-permute-start | bytes 9224
  429.2 20.1 %collective-permute-start.30 = (bf16[192,8]{0,1:T(8,128)(2,1)S(1)}, bf16[192,8]{0,1:T(8,128)(2,1)S(1)}, u32[]{:S(2)}, u32[]{:S(2)}) collective-permute-start(bf16[192,8]{0,1:T(8,128)(2,1)S(1)} %get-tuple-element.39), channel_id=1, source_target_pairs={{0,3},{1,4},{2,5},{3,6},{4,7},{5,8},{6,9},{7,10},{8,11},{9,12},{10... | collective-permute-start | bytes 9224
  431.1 22.2 %collective-permute-start.29 = (bf16[192,8]{0,1:T(8,128)(2,1)S(1)}, bf16[192,8]{0,1:T(8,128)(2,1)S(1)}, u32[]{:S(2)}, u32[]{:S(2)}) collective-permute-start(bf16[192,8]{0,1:T(8,128)(2,1)S(1)} %get-tuple-element.39), channel_id=1, source_target_pairs={{0,2},{1,3},{2,4},{3,5},{4,6},{5,7},{6,8},{7,9},{8,10},{9,11},{10,... | collective-permute-start | bytes 9224
  435.9 19.3 %collective-permute-start.28 = (bf16[192,8]{0,1:T(8,128)(2,1)S(1)}, bf16[192,8]{0,1:T(8,128)(2,1)S(1)}, u32[]{:S(2)}, u32[]{:S(2)}) collective-permute-start(bf16[192,8]{0,1:T(8,128)(2,1)S(1)} %get-tuple-element.39), channel_id=1, source_target_pairs={{0,1},{1,2},{2,3},{3,4},{4,5},{5,6},{6,7},{7,8},{8,9},{9,10},{10,1... | collective-permute-start | bytes 9224
  437.9 19.3 %collective-permute-start.27 = (bf16[192,18]{0,1:T(8,128)(2,1)S(1)}, bf16[192,18]{0,1:T(8,128)(2,1)S(1)}, u32[]{:S(2)}, u32[]{:S(2)}) collective-permute-start(bf16[192,18]{0,1:T(8,128)(2,1)S(1)} %slice.209), channel_id=1, source_target_pairs={{0,8},{1,9},{2,10},{3,11},{4,12},{5,13},{6,14},{7,15},{8,16},{9,17... | collective-permute-start | bytes 20744
  443.7 17.1 %collective-permute-start.26 = (bf16[192,24]{0,1:T(8,128)(2,1)S(1)}, bf16[192,24]{0,1:T(8,128)(2,1)S(1)}, u32[]{:S(2)}, u32[]{:S(2)}) collective-permute-start(bf16[192,24]{0,1:T(8,128)(2,1)S(1)} %get-tuple-element.36), channel_id=1, source_target_pairs={{0,7},{1,8},{2,9},{3,10},{4,11},{5,12},{6,13},{7,14},{8,15},{9,16}... | collective-permute-start | bytes 27656
  449.3 14.4 %collective-permute-start.25 = (bf16[192,24]{0,1:T(8,128)(2,1)S(1)}, bf16[192,24]{0,1:T(8,128)(2,1)S(1)}, u32[]{:S(2)}, u32[]{:S(2)}) collective-permute-start(bf16[192,24]{0,1:T(8,128)(2,1)S(1)} %get-tuple-element.36), channel_id=1, source_target_pairs={{0,6},{1,7},{2,8},{3,9},{4,10},{5,11},{6,12},{7,13},{8,14},{9,15},... | collective-permute-start | bytes 27656
  453.3 12.3 %collective-permute-start.24 = (bf16[192,24]{0,1:T(8,128)(2,1)S(1)}, bf16[192,24]{0,1:T(8,128)(2,1)S(1)}, u32[]{:S(2)}, u32[]{:S(2)}) collective-permute-start(bf16[192,24]{0,1:T(8,128)(2,1)S(1)} %get-tuple-element.36), channel_id=1, source_target_pairs={{0,5},{1,6},{2,7},{3,8},{4,9},{5,10},{6,11},{7,12},{8,13},{9,14},{... | collective-permute-start | bytes 27656
  455.2 13.7 %collective-permute-start.23 = (bf16[192,24]{0,1:T(8,128)(2,1)S(1)}, bf16[192,24]{0,1:T(8,128)(2,1)S(1)}, u32[]{:S(2)}, u32[]{:S(2)}) collective-permute-start(bf16[192,24]{0,1:T(8,128)(2,1)S(1)} %get-tuple-element.36), channel_id=1, source_target_pairs={{0,4},{1,5},{2,6},{3,7},{4,8},{5,9},{6,10},{7,11},{8,12},{9,13},{1... | collective-permute-start | bytes 27656
  457.2 13.7 %collective-permute-start.22 = (bf16[192,24]{0,1:T(8,128)(2,1)S(1)}, bf16[192,24]{0,1:T(8,128)(2,1)S(1)}, u32[]{:S(2)}, u32[]{:S(2)}) collective-permute-start(bf16[192,24]{0,1:T(8,128)(2,1)S(1)} %get-tuple-element.36), channel_id=1, source_target_pairs={{0,3},{1,4},{2,5},{3,6},{4,7},{5,8},{6,9},{7,10},{8,11},{9,12},{10... | collective-permute-start | bytes 27656
  460.9 12.0 %collective-permute-start.21 = (bf16[192,24]{0,1:T(8,128)(2,1)S(1)}, bf16[192,24]{0,1:T(8,128)(2,1)S(1)}, u32[]{:S(2)}, u32[]{:S(2)}) collective-permute-start(bf16[192,24]{0,1:T(8,128)(2,1)S(1)} %get-tuple-element.36), channel_id=1, source_target_pairs={{0,2},{1,3},{2,4},{3,5},{4,6},{5,7},{6,8},{7,9},{8,10},{9,11},{10,... | collective-permute-start | bytes 27656
  463.7 11.1 %collective-permute-start.20 = (bf16[192,24]{0,1:T(8,128)(2,1)S(1)}, bf16[192,24]{0,1:T(8,128)(2,1)S(1)}, u32[]{:S(2)}, u32[]{:S(2)}) collective-permute-start(bf16[192,24]{0,1:T(8,128)(2,1)S(1)} %get-tuple-element.36), channel_id=1, source_target_pairs={{0,1},{1,2},{2,3},{3,4},{4,5},{5,6},{6,7},{7,8},{8,9},{9,10},{10,1... | collective-permute-start | bytes 27656
  465.6 15.1 %collective-permute-start.18 = (bf16[192,24]{0,1:T(8,128)(2,1)S(1)}, bf16[192,24]{0,1:T(8,128)(2,1)S(1)}, u32[]{:S(2)}, u32[]{:S(2)}) collective-permute-start(bf16[192,24]{0,1:T(8,128)(2,1)S(1)} %get-tuple-element.37), channel_id=1, source_target_pairs={{0,7},{1,8},{2,9},{3,10},{4,11},{5,12},{6,13},{7,14},{8,15},{9,16}... | collective-permute-start | bytes 27656
  469.0 14.9 %collective-permute-start.17 = (bf16[192,24]{0,1:T(8,128)(2,1)S(1)}, bf16[192,24]{0,1:T(8,128)(2,1)S(1)}, u32[]{:S(2)}, u32[]{:S(2)}) collective-permute-start(bf16[192,24]{0,1:T(8,128)(2,1)S(1)} %get-tuple-element.37), channel_id=1, source_target_pairs={{0,6},{1,7},{2,8},{3,9},{4,10},{5,11},{6,12},{7,13},{8,14},{9,15},... | collective-permute-start | bytes 27656
  472.9 12.9 %collective-permute-start.16 = (bf16[192,24]{0,1:T(8,128)(2,1)S(1)}, bf16[192,24]{0,1:T(8,128)(2,1)S(1)}, u32[]{:S(2)}, u32[]{:S(2)}) collective-permute-start(bf16[192,24]{0,1:T(8,128)(2,1)S(1)} %get-tuple-element.37), channel_id=1, source_target_pairs={{0,5},{1,6},{2,7},{3,8},{4,9},{5,10},{6,11},{7,12},{8,13},{9,14},{... | collective-permute-start | bytes 27656
  474.8 11.0 %collective-permute-start.15 = (bf16[192,24]{0,1:T(8,128)(2,1)S(1)}, bf16[192,24]{0,1:T(8,128)(2,1)S(1)}, u32[]{:S(2)}, u32[]{:S(2)}) collective-permute-start(bf16[192,24]{0,1:T(8,128)(2,1)S(1)} %get-tuple-element.37), channel_id=1, source_target_pairs={{0,4},{1,5},{2,6},{3,7},{4,8},{5,9},{6,10},{7,11},{8,12},{9,13},{1... | collective-permute-start | bytes 27656
  (88 other events, 1031.9 us)
Sparse Core Ops, SparseCore 0:
  278.2 76.3 reduce-scatter.30
  357.3 69.7 reduce-scatter.32
  431.8 114.0 reduce-scatter.28
  550.3 116.8 reduce-scatter.26
where the time goes:
time: 751 us; the launch traced here: 741 us
  blocking collectives  237 us (32%)
  waiting for transfers between devices  193 us (26%)
  starting transfers between devices  182 us (24%)
  local copies, waits for them, and re-layouts  55.5 us (7%)
  matrix products  40.7 us (5%)
  between operations  18.5 us (2%)
  other arithmetic  14.1 us (2%)
    reduce_scatter x2, waiting for transfers between devices, reduce_grads(): lax.psum_scatter(inner_term.astype(jnp.bfloat16), 'cols', scatter_dimensi...  173 us
    unnamed x50, starting transfers between devices  139 us
    unnamed x2, blocking collectives  133 us
    psum x1, blocking collectives, local(): table_sum = lax.psum(jnp.stack([table_one, table_two]), ('rows', 'cols'))  105 us
    ppermute x6, starting transfers between devices, with_halo(): lax.ppermute(lax.slice_in_dim(block, block.shape[dim] - width, None, axis...  24 us
    unnamed x173, local copies, waits for them, and re-layouts  19 us
    ppermute x6, starting transfers between devices, with_halo(): lax.ppermute(lax.slice_in_dim(block, 0, width, axis=dim), axis, backward)  18.5 us
  transfers between devices with their start and end apart: 64, of which 13 were waited for; matrix products, arithmetic and copies ran while one was open for 6% of the time, Pallas kernels for 0%

commit v1 on v0

--- a/solution.py
+++ b/solution.py
@@ -376,7 +376,8 @@
         grad_mid_one.reshape(tile_rows, tile_cols, channels).astype(jnp.float32) + grad_tokens
     ).astype(jnp.bfloat16)
     summed_one = reduce_grads(qkv_one_grad, proj_one, inner_one, outer_one)
-    table_sum = lax.psum(jnp.stack([table_one, table_two]), ("rows", "cols"))
+    sheet = jnp.stack([table_one, table_two])
+    table_sum = lax.all_gather(sheet, ("rows", "cols")).sum(axis=0)
     qkv_grad = jnp.stack([summed_one[0], summed_two[0]])
     proj_grad = jnp.stack([summed_one[1], summed_two[1]])
     inner_grad = jnp.stack([summed_one[2], summed_two[2]])

time: 751 us -> 1140 us (1.52)
  the two profiles are of different devices: /device:TPU:16 before, /device:TPU:8 now
where the time goes in v1:
time: 1140 us; the launch traced here: 1130 us
  waiting for transfers between devices  677 us (59%)
  starting transfers between devices  176 us (15%)
  blocking collectives  139 us (12%)
  local copies, waits for them, and re-layouts  55.3 us (5%)
  matrix products  40.6 us (4%)
  between operations  20 us (2%)
  other arithmetic  18.3 us (2%)
    all_gather x1, waiting for transfers between devices, local(): table_sum = lax.all_gather(sheet, ('rows', 'cols')).sum(axis=0)  384 us
    reduce_scatter x2, waiting for transfers between devices, reduce_grads(): lax.psum_scatter(inner_term.astype(jnp.bfloat16), 'cols', scatter_dimensi...  238 us
    unnamed x2, blocking collectives  139 us
    unnamed x50, starting transfers between devices  134 us
    unnamed x55, waiting for transfers between devices  46.3 us
    ppermute x6, starting transfers between devices, with_halo(): lax.ppermute(lax.slice_in_dim(block, block.shape[dim] - width, None, axis...  23.3 us
  transfers between devices with their start and end apart: 65, of which 13 were waited for; matrix products, arithmetic and copies ran while one was open for 4% of the time, Pallas kernels for 0%

profile of v1, /device:TPU:8, one launch (start us, length us, event | category | flops | bytes accessed | tf_op | source)
XLA Modules:
  0.0 1126.1 jit_solution(16075841971525365612)
XLA Ops:
  8.8 4.3 collective-permute-start.4
  21.1 2.6 fusion.29
  27.1 2.9 multiply_convert_fusion.1
  32.6 5.5 collective-permute-start
  38.3 2.6 fusion.30
  43.7 6.0 collective-permute-start.7
  51.6 4.1 collective-permute-start.2
  55.7 3.9 collective-permute-start.3
  64.4 3.2 reshape.352
  69.2 2.4 fusion.136
  78.2 2.8 fusion.47
  91.6 2.5 copy.164
  94.1 4.0 copy.145
  98.1 5.6 convert_element_type.304
  103.7 2.6 multiply_reduce_fusion.2
  115.1 3.2 collective-permute-start.8
  118.3 4.7 collective-permute-start.9
  124.8 4.3 collective-permute-start.10
  131.2 6.1 collective-permute-done.11
  145.6 74.5 %fusion.122 = (bf16[192,24]{0,1:T(8,128)(2,1)}, bf16[192,24]{0,1:T(8,128)(2,1)}, bf16[192,8]{0,1:T(8,128)(2,1)S(1)}, bf16[192,8]{0,1:T(8,128)(2,1)S(1)}, bf16[76...) fusion(bf16[192,576]{0,1:T(8,128)(2,1)} %convolution_convert_fusion.9, ...), kind=kCustom, calls=%all-reduce-scatter.6 | all-reduce-scatter fusion | flops 786434 | bytes 1230848
  220.0 5.7 collective-permute-start.51
  225.7 3.9 collective-permute-start.50
  229.6 8.0 collective-permute-start.49
  237.6 4.6 collective-permute-start.48
  244.5 4.3 collective-permute-start.46
  248.8 2.5 collective-permute-start.45
  260.4 2.8 collective-permute-start.56
  266.1 3.7 collective-permute-start.54
  269.8 3.1 collective-permute-start.53
  277.8 2.5 collective-permute-done.52
  301.5 4.9 collective-permute-start.39
  306.4 2.8 collective-permute-start.38
  309.3 4.2 collective-permute-start.37
  315.5 4.9 collective-permute-start.34
  326.5 3.8 collective-permute-start.30
  330.3 2.8 collective-permute-start.29
  336.4 2.5 collective-permute-start.26
  348.3 3.4 collective-permute-start.22
  351.7 6.1 collective-permute-start.21
  359.7 5.9 collective-permute-start.18
  371.0 3.5 collective-permute-start.14
  374.5 2.5 collective-permute-start.13
  386.3 37.3 %reduce-scatter.33.cloned.1.call-done = bf16[48,6]{1,0:T(8,128)(2,1)} async-done(((bf16[768,6]{1,0:T(8,128)(2,1)}), bf16[48,6]{1,0:T(8,128)(2,1)}) %reduce-scatter.33.cloned.1.call-update) | async-done | bytes 592
  425.0 116.5 %reduce-scatter.29.cloned.1.call-done = bf16[192,24]{0,1:T(8,128)(2,1)} async-done(((bf16[192,768]{0,1:T(8,128)(2,1)}), bf16[192,24]{0,1:T(8,128)(2,1)}) %reduce-scatter.29.cloned.1.call-update) | async-done | bytes 9232 | tf_op jit(solution)/shard_map/reduce_scatter | solution.py:241
  541.5 121.4 %reduce-scatter.27.cloned.1.call-done = bf16[192,24]{0,1:T(8,128)(2,1)} async-done(((bf16[192,768]{0,1:T(8,128)(2,1)}), bf16[192,24]{0,1:T(8,128)(2,1)}) %reduce-scatter.27.cloned.1.call-update) | async-done | bytes 9232 | tf_op jit(solution)/shard_map/reduce_scatter | solution.py:241
  662.9 64.5 %all-reduce.19 = (bf16[192,18]{0,1:T(8,128)(2,1)S(1)}, bf16[192,18]{0,1:T(8,128)(2,1)S(1)}, bf16[192,6]{0,1:T(8,128)(2,1)S(1)}, bf16[192,6]{0,1:T(8,128)(2,1)S(1...) all-reduce(bf16[192,18]{0,1:T(8,128)(2,1)S(1)} %constant_dynamic-sl, ...), channel_id=6, replica_groups=mesh['rows'=16,'cols'=32] {'rows'}, use_global_device_ids=true, to_apply=%region_25.26.clone | all-reduce | flops 18432 | bytes 73728
  729.9 384.0 %all-gather.3.cloned.1.call-done = f32[1024,225,6]{1,2,0:T(8,128)} async-done(((f32[2,225,6]{1,2,0:T(8,128)}), f32[1024,225,6]{1,2,0:T(8,128)}) %all-gather.3.cloned.1.call-update) | async-done | bytes 5529616 | tf_op jit(solution)/shard_map/all_gather | solution.py:380
  1113.9 4.2 reduce_sum.245
  (447 shorter events, 141.9 us)
Async XLA Ops:
  8.0 377.5 %reduce-scatter.31.cloned.1.call-start = ((), (), s32[]{:S(2)}) async-start(), calls=%async_computation.7 | async-start | bytes 208896
  8.8 32.9 %collective-permute-start.4 = (bf16[4,32]{1,0:T(4,128)(2,1)S(1)}, bf16[4,32]{1,0:T(4,128)(2,1)S(1)}, u32[]{:S(2)}, u32[]{:S(2)}) collective-permute-start(bf16[4,32]{1,0:T(4,128)(2,1)S(1)} %get-tuple-element.76), channel_id=1, source_target_pairs={{0,32},{32,64},{64,96},{96,128},{128,160},{160,192},{192,224},{224... | collective-permute-start | bytes 776 | tf_op jit(solution)/shard_map/ppermute | solution.py:20
  13.1 28.6 %collective-permute-start.5 = (bf16[4,32]{1,0:T(4,128)(2,1)S(1)}, bf16[4,32]{1,0:T(4,128)(2,1)S(1)}, u32[]{:S(2)}, u32[]{:S(2)}) collective-permute-start(bf16[4,32]{1,0:T(4,128)(2,1)S(1)} %get-tuple-element.77), channel_id=1, source_target_pairs={{32,0},{64,32},{96,64},{128,96},{160,128},{192,160},{224,192},{256... | collective-permute-start | bytes 776 | tf_op jit(solution)/shard_map/ppermute | solution.py:23
  31.2 20.3 %collective-permute-start.1 = (bf16[4,32,192]{2,1,0:T(8,128)(2,1)S(1)}, bf16[4,32,192]{2,1,0:T(8,128)(2,1)S(1)}, u32[]{:S(2)}, u32[]{:S(2)}) collective-permute-start(bf16[4,32,192]{2,1,0:T(8,128)(2,1)S(1)} %bitcast.342), channel_id=1, source_target_pairs={{32,0},{64,32},{96,64},{128,96},{160,128},{192,160},{224,192},{256... | collective-permute-start | bytes 147464 | tf_op jit(solution)/shard_map/ppermute | solution.py:23
  32.6 18.9 %collective-permute-start = (bf16[4,32,192]{2,1,0:T(8,128)(2,1)S(1)}, bf16[4,32,192]{2,1,0:T(8,128)(2,1)S(1)}, u32[]{:S(2)}, u32[]{:S(2)}) collective-permute-start(bf16[4,32,192]{2,1,0:T(8,128)(2,1)S(1)} %bitcast.343), channel_id=1, source_target_pairs={{0,32},{32,64},{64,96},{96,128},{128,160},{160,192},{192,224},{224... | collective-permute-start | bytes 147464 | tf_op jit(solution)/shard_map/ppermute | solution.py:20
  220.0 24.4 %collective-permute-start.51 = (bf16[768,6]{0,1:T(8,128)(2,1)S(1)}, bf16[768,6]{0,1:T(8,128)(2,1)S(1)}, u32[]{:S(2)}, u32[]{:S(2)}) collective-permute-start(bf16[768,6]{0,1:T(8,128)(2,1)S(1)} %slice.212), channel_id=1, source_target_pairs={{0,8},{1,9},{2,10},{3,11},{4,12},{5,13},{6,14},{7,15},{8,16},{9,17... | collective-permute-start | bytes 27656
  225.7 23.1 %collective-permute-start.50 = (bf16[768,8]{0,1:T(8,128)(2,1)S(1)}, bf16[768,8]{0,1:T(8,128)(2,1)S(1)}, u32[]{:S(2)}, u32[]{:S(2)}) collective-permute-start(bf16[768,8]{0,1:T(8,128)(2,1)S(1)} %get-tuple-element.41), channel_id=1, source_target_pairs={{0,7},{1,8},{2,9},{3,10},{4,11},{5,12},{6,13},{7,14},{8,15},{9,16}... | collective-permute-start | bytes 36872
  229.6 21.7 %collective-permute-start.49 = (bf16[768,8]{0,1:T(8,128)(2,1)S(1)}, bf16[768,8]{0,1:T(8,128)(2,1)S(1)}, u32[]{:S(2)}, u32[]{:S(2)}) collective-permute-start(bf16[768,8]{0,1:T(8,128)(2,1)S(1)} %get-tuple-element.41), channel_id=1, source_target_pairs={{0,6},{1,7},{2,8},{3,9},{4,10},{5,11},{6,12},{7,13},{8,14},{9,15},... | collective-permute-start | bytes 36872
  237.6 15.6 %collective-permute-start.48 = (bf16[768,8]{0,1:T(8,128)(2,1)S(1)}, bf16[768,8]{0,1:T(8,128)(2,1)S(1)}, u32[]{:S(2)}, u32[]{:S(2)}) collective-permute-start(bf16[768,8]{0,1:T(8,128)(2,1)S(1)} %get-tuple-element.41), channel_id=1, source_target_pairs={{0,5},{1,6},{2,7},{3,8},{4,9},{5,10},{6,11},{7,12},{8,13},{9,14},{... | collective-permute-start | bytes 36872
  242.2 12.6 %collective-permute-start.47 = (bf16[768,8]{0,1:T(8,128)(2,1)S(1)}, bf16[768,8]{0,1:T(8,128)(2,1)S(1)}, u32[]{:S(2)}, u32[]{:S(2)}) collective-permute-start(bf16[768,8]{0,1:T(8,128)(2,1)S(1)} %get-tuple-element.41), channel_id=1, source_target_pairs={{0,4},{1,5},{2,6},{3,7},{4,8},{5,9},{6,10},{7,11},{8,12},{9,13},{1... | collective-permute-start | bytes 36872
  244.5 12.7 %collective-permute-start.46 = (bf16[768,8]{0,1:T(8,128)(2,1)S(1)}, bf16[768,8]{0,1:T(8,128)(2,1)S(1)}, u32[]{:S(2)}, u32[]{:S(2)}) collective-permute-start(bf16[768,8]{0,1:T(8,128)(2,1)S(1)} %get-tuple-element.41), channel_id=1, source_target_pairs={{0,3},{1,4},{2,5},{3,6},{4,7},{5,8},{6,9},{7,10},{8,11},{9,12},{10... | collective-permute-start | bytes 36872
  248.8 11.6 %collective-permute-start.45 = (bf16[768,8]{0,1:T(8,128)(2,1)S(1)}, bf16[768,8]{0,1:T(8,128)(2,1)S(1)}, u32[]{:S(2)}, u32[]{:S(2)}) collective-permute-start(bf16[768,8]{0,1:T(8,128)(2,1)S(1)} %get-tuple-element.41), channel_id=1, source_target_pairs={{0,2},{1,3},{2,4},{3,5},{4,6},{5,7},{6,8},{7,9},{8,10},{9,11},{10,... | collective-permute-start | bytes 36872
  251.3 11.9 %collective-permute-start.44 = (bf16[768,8]{0,1:T(8,128)(2,1)S(1)}, bf16[768,8]{0,1:T(8,128)(2,1)S(1)}, u32[]{:S(2)}, u32[]{:S(2)}) collective-permute-start(bf16[768,8]{0,1:T(8,128)(2,1)S(1)} %get-tuple-element.41), channel_id=1, source_target_pairs={{0,1},{1,2},{2,3},{3,4},{4,5},{5,6},{6,7},{7,8},{8,9},{9,10},{10,1... | collective-permute-start | bytes 36872
  253.2 16.5 %collective-permute-start.58 = (bf16[768,8]{0,1:T(8,128)(2,1)S(1)}, bf16[768,8]{0,1:T(8,128)(2,1)S(1)}, u32[]{:S(2)}, u32[]{:S(2)}) collective-permute-start(bf16[768,8]{0,1:T(8,128)(2,1)S(1)} %get-tuple-element.40), channel_id=1, source_target_pairs={{0,7},{1,8},{2,9},{3,10},{4,11},{5,12},{6,13},{7,14},{8,15},{9,16}... | collective-permute-start | bytes 36872
  254.9 18.0 %collective-permute-start.57 = (bf16[768,8]{0,1:T(8,128)(2,1)S(1)}, bf16[768,8]{0,1:T(8,128)(2,1)S(1)}, u32[]{:S(2)}, u32[]{:S(2)}) collective-permute-start(bf16[768,8]{0,1:T(8,128)(2,1)S(1)} %get-tuple-element.40), channel_id=1, source_target_pairs={{0,6},{1,7},{2,8},{3,9},{4,10},{5,11},{6,12},{7,13},{8,14},{9,15},... | collective-permute-start | bytes 36872
  260.4 15.4 %collective-permute-start.56 = (bf16[768,8]{0,1:T(8,128)(2,1)S(1)}, bf16[768,8]{0,1:T(8,128)(2,1)S(1)}, u32[]{:S(2)}, u32[]{:S(2)}) collective-permute-start(bf16[768,8]{0,1:T(8,128)(2,1)S(1)} %get-tuple-element.40), channel_id=1, source_target_pairs={{0,5},{1,6},{2,7},{3,8},{4,9},{5,10},{6,11},{7,12},{8,13},{9,14},{... | collective-permute-start | bytes 36872
  263.2 12.6 %collective-permute-start.55 = (bf16[768,8]{0,1:T(8,128)(2,1)S(1)}, bf16[768,8]{0,1:T(8,128)(2,1)S(1)}, u32[]{:S(2)}, u32[]{:S(2)}) collective-permute-start(bf16[768,8]{0,1:T(8,128)(2,1)S(1)} %get-tuple-element.40), channel_id=1, source_target_pairs={{0,4},{1,5},{2,6},{3,7},{4,8},{5,9},{6,10},{7,11},{8,12},{9,13},{1... | collective-permute-start | bytes 36872
  266.1 9.7 collective-permute-start.54
  275.8 147.8 %reduce-scatter.33.cloned.1.call-start = ((), (), s32[]{:S(2)}) async-start(), calls=%async_computation.8 | async-start | bytes 208896
  282.1 259.4 %reduce-scatter.29.cloned.1.call-start = ((), (), s32[]{:S(2)}) async-start(), calls=%async_computation.5 | async-start | bytes 405504 | tf_op jit(solution)/shard_map/reduce_scatter | solution.py:241
  283.3 379.6 %reduce-scatter.27.cloned.1.call-start = ((), (), s32[]{:S(2)}) async-start(), calls=%async_computation.4 | async-start | bytes 405504 | tf_op jit(solution)/shard_map/reduce_scatter | solution.py:241
  284.9 829.0 %all-gather.3.cloned.1.call-start = ((), (), s32[]{:S(2)}) async-start(), calls=%async_computation.6 | async-start | bytes 8404992 | tf_op jit(solution)/shard_map/all_gather | solution.py:380
  291.2 18.1 %collective-permute-start.42 = (bf16[192,8]{0,1:T(8,128)(2,1)S(1)}, bf16[192,8]{0,1:T(8,128)(2,1)S(1)}, u32[]{:S(2)}, u32[]{:S(2)}) collective-permute-start(bf16[192,8]{0,1:T(8,128)(2,1)S(1)} %get-tuple-element.38), channel_id=1, source_target_pairs={{0,7},{1,8},{2,9},{3,10},{4,11},{5,12},{6,13},{7,14},{8,15},{9,16}... | collective-permute-start | bytes 9224
  292.6 20.9 %collective-permute-start.41 = (bf16[192,8]{0,1:T(8,128)(2,1)S(1)}, bf16[192,8]{0,1:T(8,128)(2,1)S(1)}, u32[]{:S(2)}, u32[]{:S(2)}) collective-permute-start(bf16[192,8]{0,1:T(8,128)(2,1)S(1)} %get-tuple-element.38), channel_id=1, source_target_pairs={{0,6},{1,7},{2,8},{3,9},{4,10},{5,11},{6,12},{7,13},{8,14},{9,15},... | collective-permute-start | bytes 9224
  294.2 21.3 %collective-permute-start.40 = (bf16[192,8]{0,1:T(8,128)(2,1)S(1)}, bf16[192,8]{0,1:T(8,128)(2,1)S(1)}, u32[]{:S(2)}, u32[]{:S(2)}) collective-permute-start(bf16[192,8]{0,1:T(8,128)(2,1)S(1)} %get-tuple-element.38), channel_id=1, source_target_pairs={{0,5},{1,6},{2,7},{3,8},{4,9},{5,10},{6,11},{7,12},{8,13},{9,14},{... | collective-permute-start | bytes 9224
  301.5 18.9 %collective-permute-start.39 = (bf16[192,8]{0,1:T(8,128)(2,1)S(1)}, bf16[192,8]{0,1:T(8,128)(2,1)S(1)}, u32[]{:S(2)}, u32[]{:S(2)}) collective-permute-start(bf16[192,8]{0,1:T(8,128)(2,1)S(1)} %get-tuple-element.38), channel_id=1, source_target_pairs={{0,4},{1,5},{2,6},{3,7},{4,8},{5,9},{6,10},{7,11},{8,12},{9,13},{1... | collective-permute-start | bytes 9224
  306.4 15.3 %collective-permute-start.38 = (bf16[192,8]{0,1:T(8,128)(2,1)S(1)}, bf16[192,8]{0,1:T(8,128)(2,1)S(1)}, u32[]{:S(2)}, u32[]{:S(2)}) collective-permute-start(bf16[192,8]{0,1:T(8,128)(2,1)S(1)} %get-tuple-element.38), channel_id=1, source_target_pairs={{0,3},{1,4},{2,5},{3,6},{4,7},{5,8},{6,9},{7,10},{8,11},{9,12},{10... | collective-permute-start | bytes 9224
  309.3 15.0 %collective-permute-start.37 = (bf16[192,8]{0,1:T(8,128)(2,1)S(1)}, bf16[192,8]{0,1:T(8,128)(2,1)S(1)}, u32[]{:S(2)}, u32[]{:S(2)}) collective-permute-start(bf16[192,8]{0,1:T(8,128)(2,1)S(1)} %get-tuple-element.38), channel_id=1, source_target_pairs={{0,2},{1,3},{2,4},{3,5},{4,6},{5,7},{6,8},{7,9},{8,10},{9,11},{10,... | collective-permute-start | bytes 9224
  313.5 13.0 %collective-permute-start.36 = (bf16[192,8]{0,1:T(8,128)(2,1)S(1)}, bf16[192,8]{0,1:T(8,128)(2,1)S(1)}, u32[]{:S(2)}, u32[]{:S(2)}) collective-permute-start(bf16[192,8]{0,1:T(8,128)(2,1)S(1)} %get-tuple-element.38), channel_id=1, source_target_pairs={{0,1},{1,2},{2,3},{3,4},{4,5},{5,6},{6,7},{7,8},{8,9},{9,10},{10,1... | collective-permute-start | bytes 9224
  315.5 14.8 %collective-permute-start.34 = (bf16[192,8]{0,1:T(8,128)(2,1)S(1)}, bf16[192,8]{0,1:T(8,128)(2,1)S(1)}, u32[]{:S(2)}, u32[]{:S(2)}) collective-permute-start(bf16[192,8]{0,1:T(8,128)(2,1)S(1)} %get-tuple-element.39), channel_id=1, source_target_pairs={{0,7},{1,8},{2,9},{3,10},{4,11},{5,12},{6,13},{7,14},{8,15},{9,16}... | collective-permute-start | bytes 9224
  320.4 12.6 %collective-permute-start.33 = (bf16[192,8]{0,1:T(8,128)(2,1)S(1)}, bf16[192,8]{0,1:T(8,128)(2,1)S(1)}, u32[]{:S(2)}, u32[]{:S(2)}) collective-permute-start(bf16[192,8]{0,1:T(8,128)(2,1)S(1)} %get-tuple-element.39), channel_id=1, source_target_pairs={{0,6},{1,7},{2,8},{3,9},{4,10},{5,11},{6,12},{7,13},{8,14},{9,15},... | collective-permute-start | bytes 9224
  321.8 13.2 %collective-permute-start.32 = (bf16[192,8]{0,1:T(8,128)(2,1)S(1)}, bf16[192,8]{0,1:T(8,128)(2,1)S(1)}, u32[]{:S(2)}, u32[]{:S(2)}) collective-permute-start(bf16[192,8]{0,1:T(8,128)(2,1)S(1)} %get-tuple-element.39), channel_id=1, source_target_pairs={{0,5},{1,6},{2,7},{3,8},{4,9},{5,10},{6,11},{7,12},{8,13},{9,14},{... | collective-permute-start | bytes 9224
  324.3 12.2 %collective-permute-start.31 = (bf16[192,8]{0,1:T(8,128)(2,1)S(1)}, bf16[192,8]{0,1:T(8,128)(2,1)S(1)}, u32[]{:S(2)}, u32[]{:S(2)}) collective-permute-start(bf16[192,8]{0,1:T(8,128)(2,1)S(1)} %get-tuple-element.39), channel_id=1, source_target_pairs={{0,4},{1,5},{2,6},{3,7},{4,8},{5,9},{6,10},{7,11},{8,12},{9,13},{1... | collective-permute-start | bytes 9224
  326.5 12.5 %collective-permute-start.30 = (bf16[192,8]{0,1:T(8,128)(2,1)S(1)}, bf16[192,8]{0,1:T(8,128)(2,1)S(1)}, u32[]{:S(2)}, u32[]{:S(2)}) collective-permute-start(bf16[192,8]{0,1:T(8,128)(2,1)S(1)} %get-tuple-element.39), channel_id=1, source_target_pairs={{0,3},{1,4},{2,5},{3,6},{4,7},{5,8},{6,9},{7,10},{8,11},{9,12},{10... | collective-permute-start | bytes 9224
  330.3 10.9 collective-permute-start.29
  333.0 10.4 collective-permute-start.28
  335.0 10.4 collective-permute-start.19
  336.4 15.3 %collective-permute-start.26 = (bf16[192,24]{0,1:T(8,128)(2,1)S(1)}, bf16[192,24]{0,1:T(8,128)(2,1)S(1)}, u32[]{:S(2)}, u32[]{:S(2)}) collective-permute-start(bf16[192,24]{0,1:T(8,128)(2,1)S(1)} %copy-done.53), channel_id=1, source_target_pairs={{0,7},{1,8},{2,9},{3,10},{4,11},{5,12},{6,13},{7,14},{8,15},{9,16}... | collective-permute-start | bytes 27656
  339.0 18.8 %collective-permute-start.25 = (bf16[192,24]{0,1:T(8,128)(2,1)S(1)}, bf16[192,24]{0,1:T(8,128)(2,1)S(1)}, u32[]{:S(2)}, u32[]{:S(2)}) collective-permute-start(bf16[192,24]{0,1:T(8,128)(2,1)S(1)} %copy-done.53), channel_id=1, source_target_pairs={{0,6},{1,7},{2,8},{3,9},{4,10},{5,11},{6,12},{7,13},{8,14},{9,15},... | collective-permute-start | bytes 27656
  341.2 18.5 %collective-permute-start.24 = (bf16[192,24]{0,1:T(8,128)(2,1)S(1)}, bf16[192,24]{0,1:T(8,128)(2,1)S(1)}, u32[]{:S(2)}, u32[]{:S(2)}) collective-permute-start(bf16[192,24]{0,1:T(8,128)(2,1)S(1)} %copy-done.53), channel_id=1, source_target_pairs={{0,5},{1,6},{2,7},{3,8},{4,9},{5,10},{6,11},{7,12},{8,13},{9,14},{... | collective-permute-start | bytes 27656
  343.4 22.2 %collective-permute-start.23 = (bf16[192,24]{0,1:T(8,128)(2,1)S(1)}, bf16[192,24]{0,1:T(8,128)(2,1)S(1)}, u32[]{:S(2)}, u32[]{:S(2)}) collective-permute-start(bf16[192,24]{0,1:T(8,128)(2,1)S(1)} %copy-done.53), channel_id=1, source_target_pairs={{0,4},{1,5},{2,6},{3,7},{4,8},{5,9},{6,10},{7,11},{8,12},{9,13},{1... | collective-permute-start | bytes 27656
  348.3 19.5 %collective-permute-start.22 = (bf16[192,24]{0,1:T(8,128)(2,1)S(1)}, bf16[192,24]{0,1:T(8,128)(2,1)S(1)}, u32[]{:S(2)}, u32[]{:S(2)}) collective-permute-start(bf16[192,24]{0,1:T(8,128)(2,1)S(1)} %copy-done.53), channel_id=1, source_target_pairs={{0,3},{1,4},{2,5},{3,6},{4,7},{5,8},{6,9},{7,10},{8,11},{9,12},{10... | collective-permute-start | bytes 27656
  351.7 17.3 %collective-permute-start.21 = (bf16[192,24]{0,1:T(8,128)(2,1)S(1)}, bf16[192,24]{0,1:T(8,128)(2,1)S(1)}, u32[]{:S(2)}, u32[]{:S(2)}) collective-permute-start(bf16[192,24]{0,1:T(8,128)(2,1)S(1)} %copy-done.53), channel_id=1, source_target_pairs={{0,2},{1,3},{2,4},{3,5},{4,6},{5,7},{6,8},{7,9},{8,10},{9,11},{10,... | collective-permute-start | bytes 27656
  357.8 13.2 %collective-permute-start.20 = (bf16[192,24]{0,1:T(8,128)(2,1)S(1)}, bf16[192,24]{0,1:T(8,128)(2,1)S(1)}, u32[]{:S(2)}, u32[]{:S(2)}) collective-permute-start(bf16[192,24]{0,1:T(8,128)(2,1)S(1)} %copy-done.53), channel_id=1, source_target_pairs={{0,1},{1,2},{2,3},{3,4},{4,5},{5,6},{6,7},{7,8},{8,9},{9,10},{10,1... | collective-permute-start | bytes 27656
  359.7 14.7 %collective-permute-start.18 = (bf16[192,24]{0,1:T(8,128)(2,1)S(1)}, bf16[192,24]{0,1:T(8,128)(2,1)S(1)}, u32[]{:S(2)}, u32[]{:S(2)}) collective-permute-start(bf16[192,24]{0,1:T(8,128)(2,1)S(1)} %copy-done.52), channel_id=1, source_target_pairs={{0,7},{1,8},{2,9},{3,10},{4,11},{5,12},{6,13},{7,14},{8,15},{9,16}... | collective-permute-start | bytes 27656
  365.6 11.3 %collective-permute-start.17 = (bf16[192,24]{0,1:T(8,128)(2,1)S(1)}, bf16[192,24]{0,1:T(8,128)(2,1)S(1)}, u32[]{:S(2)}, u32[]{:S(2)}) collective-permute-start(bf16[192,24]{0,1:T(8,128)(2,1)S(1)} %copy-done.52), channel_id=1, source_target_pairs={{0,6},{1,7},{2,8},{3,9},{4,10},{5,11},{6,12},{7,13},{8,14},{9,15},... | collective-permute-start | bytes 27656
  367.8 12.3 %collective-permute-start.16 = (bf16[192,24]{0,1:T(8,128)(2,1)S(1)}, bf16[192,24]{0,1:T(8,128)(2,1)S(1)}, u32[]{:S(2)}, u32[]{:S(2)}) collective-permute-start(bf16[192,24]{0,1:T(8,128)(2,1)S(1)} %copy-done.52), channel_id=1, source_target_pairs={{0,5},{1,6},{2,7},{3,8},{4,9},{5,10},{6,11},{7,12},{8,13},{9,14},{... | collective-permute-start | bytes 27656
  369.1 11.0 collective-permute-start.15
  (95 other events, 1165.8 us)
Sparse Core Ops, SparseCore 0:
  275.9 74.5 reduce-scatter.30
  353.3 70.2 reduce-scatter.32
  428.2 113.2 reduce-scatter.28
  545.9 116.9 reduce-scatter.26
Sparse Core Ops, SparseCore 1:
  288.7 825.2 all-gather.2
